TPU v7x, 32 devices: a whole 2x2x4 slice. The times are simulated.
32 devices in a mesh: member: 2 (over x), ty: 16 (over z, y, core).
Axes of the slice: x: 2, y: 2, z: 4, core: 2. Of those that a mesh axis runs over, the one named last changes fastest.
Arguments:
- fields: float32 [32, 768, 6, 768], P('member', 'ty'), parts along dimension 0, may hold values from -6 to 6
- damp_four: float32 [32], P('member'), parts along dimension 0, may hold values from 0.004 to 0.03
- damp_six: float32 [32], P('member'), parts along dimension 0, may hold values from 0.0008 to 0.006
- metric: float32 [4, 768, 6, 768], P(None, 'ty'), may hold values from 0.1 to 1.9
- seam_table: int32 [6, 4, 3], replicated, may hold values from 0 to 5
Outputs:
- damped: float32 [32, 768, 6, 768], P('member', 'ty'), parts along dimension 0
There are 2 independent parts, one for each index of `member`. A program takes and returns all parts, laid end to end along the dimension named above; an argument that names none is the same for every part. Nothing has to cross between parts.
Inputs may be any that keep to these rules, and one draw needn't show every extreme that they name: The table describes the surface of a cube with every face seen from outside: the joining is symmetric, no face is joined to itself, and r is 1 exactly when both edges are among (south, east) or both among (north, west).
All inputs are finite; a program needn't handle non-finite values.
Results may differ from a plain program's by a relative error of at most 0.00005.
Values sent between devices are 32-bit elements; how exact they have to be, the bound alone decides.
A program may use at most 128 MiB of HBM per device.

v0:
```python
import jax
import jax.numpy as jnp
from jax import lax
from jax.sharding import PartitionSpec as P


def with_halo(cells, sides, width):
    for axis, dim in sides:
        count = lax.axis_size(axis)
        ends = count - 1
        head = lax.slice_in_dim(cells, 0, width, axis=dim)
        tail = lax.slice_in_dim(cells, cells.shape[dim] - width, cells.shape[dim], axis=dim)
        cells = jnp.concatenate(
            [
                lax.ppermute(tail, axis, [(i, (i + 1) % count) for i in range(ends)]),
                cells,
                lax.ppermute(head, axis, [((i + 1) % count, i) for i in range(ends)]),
            ],
            axis=dim,
        )
    return cells


def strip_edges(source):
    east_cells = jnp.transpose(source[:, :, :, -1], (0, 2, 1))
    west_cells = jnp.transpose(source[:, :, :, 0], (0, 2, 1))
    return jnp.stack([east_cells, west_cells], axis=2)


def gather_edges(source):
    tile_index = lax.axis_index("ty")
    tile_count = lax.axis_size("ty")
    strip_rows = source.shape[1]
    row_width = source.shape[3]
    strip_cells = strip_edges(source)
    first_row = jnp.where(tile_index == 0, source[:, 0], 0.0)
    last_row = jnp.where(tile_index == tile_count - 1, source[:, -1], 0.0)
    blank = jnp.zeros(strip_cells.shape[:3] + (row_width,), jnp.float32)
    placed = lax.dynamic_update_slice_in_dim(blank, strip_cells, tile_index * strip_rows, 3)
    rim_cells = jnp.stack([first_row, placed[:, :, 0], last_row, placed[:, :, 1]], axis=2)
    edge_set = lax.psum(rim_cells, "ty")
    return edge_set


def seam_halo(edge_set, seam_table):
    levels = edge_set.shape[0]
    row_width = edge_set.shape[3]
    flattened = edge_set.reshape(levels, 24, row_width)
    picked = (seam_table[:, :, 0] * 4 + seam_table[:, :, 1]).reshape(24)
    onehot = (picked[:, None] == jnp.arange(24, dtype=jnp.int32)[None, :]).astype(jnp.float32)
    neighbor = jnp.einsum("jk,lkc->ljc", onehot, flattened, precision=lax.Precision.HIGHEST)
    neighbor = neighbor.reshape(levels, 6, 4, row_width)
    flipped = (seam_table[:, :, 2] == 1)[None, :, :, None]
    return jnp.where(flipped, neighbor[..., ::-1], neighbor)


def laplace(source, metric, seam_table):
    tile_index = lax.axis_index("ty")
    tile_count = lax.axis_size("ty")
    strip_rows = source.shape[1]
    padded = with_halo(source, (("ty", 1),), 1)
    halo_cells = seam_halo(gather_edges(source), seam_table)
    south_row = jnp.where(tile_index == 0, halo_cells[:, :, 0], padded[:, 0])
    north_row = jnp.where(tile_index == tile_count - 1, halo_cells[:, :, 2], padded[:, -1])
    row_start = tile_index * strip_rows
    west_cells = jnp.transpose(
        lax.dynamic_slice_in_dim(halo_cells[:, :, 3], row_start, strip_rows, 2), (0, 2, 1)
    )[..., None]
    east_cells = jnp.transpose(
        lax.dynamic_slice_in_dim(halo_cells[:, :, 1], row_start, strip_rows, 2), (0, 2, 1)
    )[..., None]
    padded_x = jnp.concatenate([west_cells, source, east_cells], axis=3)
    padded_y = jnp.concatenate([south_row[:, None], source, north_row[:, None]], axis=1)
    return (
        metric[0] * (padded_x[..., :-2] - source)
        + metric[1] * (padded_x[..., 2:] - source)
        + metric[2] * (padded_y[:, :-2] - source)
        + metric[3] * (padded_y[:, 2:] - source)
    )


def per_device(fields, damp_four, damp_six, metric, seam_table):
    second = laplace(fields, metric, seam_table)
    fourth = laplace(second, metric, seam_table)
    sixth = laplace(fourth, metric, seam_table)
    return fields - damp_four[:, None, None, None] * fourth + damp_six[:, None, None, None] * sixth


def solution(mesh):
    placed = (
        P("member", "ty", None, None),
        P("member"),
        P("member"),
        P(None, "ty", None, None),
        P(),
    )
    return jax.shard_map(
        per_device,
        mesh=mesh,
        in_specs=placed,
        out_specs=P("member", "ty", None, None),
        check_vma=False,
    )
```

profile of v0, /device:TPU:0, one launch (start us, length us, event | category | flops | bytes accessed | tf_op | source)
XLA Modules:
  0.0 596.8 jit_solution(6882728278029485408)
XLA Ops:
  6.5 4.6 fusion.54
  11.1 18.5 %copy.89 = f32[16,48,6,768]{3,0,2,1:T(8,128)} copy(f32[16,48,6,768]{3,1,2,0:T(8,128)} %param.5) | data formatting | bytes 28311552 | tf_op args[0]
  29.6 2.5 copy.101
  33.7 2.0 fusion.53
  36.6 1.4 reshape.130
  38.1 4.7 collective-permute-start
  42.8 1.3 collective-permute-start.1
  44.4 2.2 slice_bitcast_fusion.3
  48.2 1.6 copy.79
  49.8 88.0 %all-reduce.4.cloned.1.call-done = f32[16,24,768]{2,1,0:T(8,128)} async-done(((f32[16,24,768]{2,1,0:T(8,128)}), f32[16,24,768]{2,1,0:T(8,128)}) %all-reduce.4.cloned.1.call-update) | async-done | bytes 1179664 | tf_op jit(solution)/shard_map/psum | solution.py:41
  137.8 1.9 convolution_bitcast_fusion.2
  139.7 1.4 copy.100
  141.1 4.7 rev.9
  145.8 1.8 broadcast_select_fusion
  150.1 3.9 copy.68
  154.1 1.6 dynamic-slice_bitcast_fusion.4
  155.7 4.0 copy.73
  159.7 2.0 fusion.40
  161.7 33.4 %fusion.26 = f32[16,48,6,768]{3,0,2,1:T(8,128)} fusion(f32[16,48,6,768]{3,0,2,1:T(8,128)} %copy.89, f32[16,1,6,768]{3,0,2,1:T(8,128)} %get-tuple-element.38, f32[16,1,6,768]{3,0,2,1:T(8,128)} %get-tuple-element.37, f32[16,48,6,1]{3,0,2,1:T(8,128)} %copy.73, f32[16,48,6,1]{3,0,2,1:T(8,128)} %copy.68, f32[48,6,768]{2,1,0:T(8,128)} %copy.79, ...), kind=kLoop, calls=%fused_computation.35 | loop fusion | flops 53084160 | bytes 32477184 | tf_op jit(solution)/shard_map/add | solution.py:75
  195.1 5.3 fusion.52
  200.4 2.1 fusion.51
  202.5 3.4 copy.104
  205.9 3.4 copy.83
  209.3 1.5 pad_maximum_fusion.16
  211.7 1.7 dynamic_update_slice.10
  213.4 1.1 fusion.59
  214.5 1.1 pad_maximum_fusion.13
  215.6 1.8 copy.84
  217.4 2.6 reshape.132
  220.1 3.2 collective-permute-start.2
  223.3 1.3 collective-permute-start.3
  224.6 91.8 %all-reduce.6.cloned.1.call-done = f32[16,24,768]{2,1,0:T(8,128)} async-done(((f32[16,24,768]{2,1,0:T(8,128)}), f32[16,24,768]{2,1,0:T(8,128)}) %all-reduce.6.cloned.1.call-update) | async-done | bytes 1179664 | tf_op jit(solution)/shard_map/psum | solution.py:41
  316.4 3.0 convolution_bitcast_fusion.1
  319.3 10.9 %reshape.133 = f32[16,6,4,768]{3,2,1,0:T(4,128)} reshape(f32[16,24,768]{2,1,0:T(8,128)} %convolution_bitcast_fusion.1) | data formatting | bytes 2359296 | tf_op jit(solution)/shard_map/reshape | solution.py:52
  330.3 2.7 copy.85
  332.9 4.7 rev.10
  337.6 2.0 broadcast_select_fusion.1
  342.1 3.9 copy.87
  346.1 1.6 dynamic-slice_bitcast_fusion.2
  347.7 4.0 copy.88
  351.7 2.0 fusion.38
  353.7 34.7 %fusion.15 = f32[16,48,6,768]{3,0,2,1:T(8,128)} fusion(f32[16,48,6,768]{3,0,2,1:T(8,128)} %fusion.26, f32[16,1,6,768]{3,0,2,1:T(8,128)} %get-tuple-element.34, f32[16,1,6,768]{3,0,2,1:T(8,128)} %get-tuple-element.33, f32[16,48,6,1]{3,0,2,1:T(8,128)} %copy.88, f32[16,48,6,1]{3,0,2,1:T(8,128)} %copy.87, f32[48,6,768]{2,1,0:T(8,128)} %copy.79, ...), kind=kLoop, calls=%fused_computation.20 | loop fusion | flops 53084160 | bytes 32477184 | tf_op jit(solution)/shard_map/add | solution.py:75
  388.4 5.3 fusion.50
  393.7 2.1 fusion.49
  395.8 3.4 copy.90
  399.2 3.4 copy.91
  402.6 1.5 pad_maximum_fusion.17
  405.0 1.7 dynamic_update_slice.11
  407.8 1.1 pad_maximum_fusion.14
  408.9 1.8 copy.94
  410.7 2.8 reshape.134
  413.6 3.2 collective-permute-start.4
  416.8 1.3 collective-permute-start.5
  418.1 91.7 %all-reduce.8.cloned.1.call-done = f32[16,24,768]{2,1,0:T(8,128)} async-done(((f32[16,24,768]{2,1,0:T(8,128)}), f32[16,24,768]{2,1,0:T(8,128)}) %all-reduce.8.cloned.1.call-update) | async-done | bytes 1179664 | tf_op jit(solution)/shard_map/psum | solution.py:41
  509.8 3.0 convolution_bitcast_fusion
  512.7 2.6 reshape.135
  515.3 2.7 copy.95
  518.0 4.7 rev.11
  522.7 2.0 broadcast_select_fusion.2
  526.5 3.9 copy.97
  530.5 4.0 copy.98
  534.5 1.3 fusion.36
  536.0 35.3 %fusion.4 = f32[16,48,6,768]{3,0,2,1:T(8,128)} fusion(f32[16,48,6,768]{3,0,2,1:T(8,128)} %fusion.15, f32[16,1,6,768]{3,0,2,1:T(8,128)S(1)} %get-tuple-element.30, f32[16,1,6,768]{3,0,2,1:T(8,128)S(1)} %get-tuple-element.29, f32[16,48,6,1]{3,0,2,1:T(8,128)} %copy.98, f32[16,48,6,1]{3,0,2,1:T(8,128)} %copy.97, f32[16]{0:T(128)S(1)} %copy-done.5, ...), kind=kLoop, calls=%fused_computation.5 | loop fusion | flops 67239936 | bytes 46633088 | tf_op jit(solution)/shard_map/add | solution.py:86
  571.3 18.5 %copy.99 = f32[16,48,6,768]{3,1,2,0:T(8,128)} copy(f32[16,48,6,768]{3,0,2,1:T(8,128)} %fusion.4) | data formatting | bytes 28311552 | tf_op jit(solution)/shard_map/add | solution.py:86
  (51 shorter events, 14.2 us)
Async XLA Ops:
  6.5 131.3 %all-reduce.4.cloned.1.call-start = ((), (), s32[]{:S(2)}) async-start(), calls=%async_computation | async-start | bytes 2359296 | tf_op jit(solution)/shard_map/psum | solution.py:41
  36.6 7.5 %copy-start.4 = (s32[6,4,3]{0,1,2:T(4,128)S(1)}, s32[6,4,3]{0,1,2:T(4,128)}, u32[]{:S(2)}) copy-start(s32[6,4,3]{0,1,2:T(4,128)} %param.9) | copy-start | bytes 868
  38.0 278.3 %all-reduce.6.cloned.1.call-start = ((), (), s32[]{:S(2)}) async-start(), calls=%async_computation.1 | async-start | bytes 2359296 | tf_op jit(solution)/shard_map/psum | solution.py:41
  38.1 121.6 %collective-permute-start = (f32[16,1,6,768]{3,0,2,1:T(8,128)}, f32[16,1,6,768]{3,0,2,1:T(8,128)}, u32[]{:S(2)}, u32[]{:S(2)}) collective-permute-start(f32[16,1,6,768]{3,0,2,1:T(8,128)} %get-tuple-element.17), channel_id=1, source_target_pairs={{0,1},{1,2},{2,3},{3,4},{4,5},{5,6},{6,7},{7,8},{8,9},{9,10},{10,1... | collective-permute-start | bytes 884744 | tf_op jit(solution)/shard_map/ppermute | solution.py:15
  42.8 116.8 %collective-permute-start.1 = (f32[16,1,6,768]{3,0,2,1:T(8,128)}, f32[16,1,6,768]{3,0,2,1:T(8,128)}, u32[]{:S(2)}, u32[]{:S(2)}) collective-permute-start(f32[16,1,6,768]{3,0,2,1:T(8,128)} %get-tuple-element.19), channel_id=1, source_target_pairs={{1,0},{2,1},{3,2},{4,3},{5,4},{6,5},{7,6},{8,7},{9,8},{10,9},{11,1... | collective-permute-start | bytes 884744 | tf_op jit(solution)/shard_map/ppermute | solution.py:17
  147.7 1.0 copy-start.2
  220.0 289.8 %all-reduce.8.cloned.1.call-start = ((), (), s32[]{:S(2)}) async-start(), calls=%async_computation.2 | async-start | bytes 2359296 | tf_op jit(solution)/shard_map/psum | solution.py:41
  220.1 131.6 %collective-permute-start.2 = (f32[16,1,6,768]{3,0,2,1:T(8,128)}, f32[16,1,6,768]{3,0,2,1:T(8,128)}, u32[]{:S(2)}, u32[]{:S(2)}) collective-permute-start(f32[16,1,6,768]{3,0,2,1:T(8,128)} %get-tuple-element.11), channel_id=1, source_target_pairs={{0,1},{1,2},{2,3},{3,4},{4,5},{5,6},{6,7},{7,8},{8,9},{9,10},{10,1... | collective-permute-start | bytes 884744 | tf_op jit(solution)/shard_map/ppermute | solution.py:15
  223.3 128.3 %collective-permute-start.3 = (f32[16,1,6,768]{3,0,2,1:T(8,128)}, f32[16,1,6,768]{3,0,2,1:T(8,128)}, u32[]{:S(2)}, u32[]{:S(2)}) collective-permute-start(f32[16,1,6,768]{3,0,2,1:T(8,128)} %get-tuple-element.14), channel_id=1, source_target_pairs={{1,0},{2,1},{3,2},{4,3},{5,4},{6,5},{7,6},{8,7},{9,8},{10,9},{11,1... | collective-permute-start | bytes 884744 | tf_op jit(solution)/shard_map/ppermute | solution.py:17
  339.7 1.0 copy-start.3
  413.6 120.9 %collective-permute-start.4 = (f32[16,1,6,768]{3,0,2,1:T(8,128)}, f32[16,1,6,768]{3,0,2,1:T(8,128)}, u32[]{:S(2)}, u32[]{:S(2)}) collective-permute-start(f32[16,1,6,768]{3,0,2,1:T(8,128)} %get-tuple-element.5), channel_id=1, source_target_pairs={{0,1},{1,2},{2,3},{3,4},{4,5},{5,6},{6,7},{7,8},{8,9},{9,10},{10,1... | collective-permute-start | bytes 884744 | tf_op jit(solution)/shard_map/ppermute | solution.py:15
  416.8 117.7 %collective-permute-start.5 = (f32[16,1,6,768]{3,0,2,1:T(8,128)}, f32[16,1,6,768]{3,0,2,1:T(8,128)}, u32[]{:S(2)}, u32[]{:S(2)}) collective-permute-start(f32[16,1,6,768]{3,0,2,1:T(8,128)} %get-tuple-element.8), channel_id=1, source_target_pairs={{1,0},{2,1},{3,2},{4,3},{5,4},{6,5},{7,6},{8,7},{9,8},{10,9},{11,1... | collective-permute-start | bytes 884744 | tf_op jit(solution)/shard_map/ppermute | solution.py:17
  524.7 1.0 copy-start.1
  530.5 5.4 copy-start.5
  530.5 5.4 copy-start.6
  534.5 1.5 copy-start
Sparse Core Ops, SparseCore 0:
  38.2 99.5 all-reduce.3
  220.1 96.1 all-reduce.5
  413.7 96.0 all-reduce.7
where the time goes:
time: 606 us; the launch traced here: 597 us
  waiting for transfers between devices  271 us (45%)
  local copies, waits for them, and re-layouts  162 us (27%)
  other arithmetic  126 us (21%)
  starting transfers between devices  15.1 us (2%)
  between operations  13.8 us (2%)
  matrix products  7.85 us (1%)
    psum x3, waiting for transfers between devices, gather_edges(): edge_set = lax.psum(rim_cells, 'ty')  271 us
    add x2, other arithmetic, laplace(): metric[0] * (padded_x[..., :-2] - source)  68.1 us
    add x1, other arithmetic, per_device(): fields - damp_four[:, None, None, None] * fourth  35.3 us
    unnamed x19, local copies, waits for them, and re-layouts  28.6 us
    reshape x5, local copies, waits for them, and re-layouts, seam_halo(): neighbor = neighbor.reshape(levels, 6, 4, row_width)  20.2 us
    slice x4, local copies, waits for them, and re-layouts, strip_edges(): east_cells = jnp.transpose(source[:, :, :, -1], (0, 2, 1))  18.6 us
    add x1, local copies, waits for them, and re-layouts, per_device(): fields - damp_four[:, None, None, None] * fourth  18.5 us
    broadcast_in_dim x6, local copies, waits for them, and re-layouts, laplace(): jnp.transpose(lax.dynamic_slice_in_dim(halo_cells[:, :, 1], row_start, st...  15.9 us
  transfers between devices with their start and end apart: 9, of which 3 were waited for; matrix products, arithmetic and copies ran while one was open for 14% of the time, Pallas kernels for 0%

commit v1 on v0

--- a/solution.py
+++ b/solution.py
@@ -38,7 +38,7 @@
     blank = jnp.zeros(strip_cells.shape[:3] + (row_width,), jnp.float32)
     placed = lax.dynamic_update_slice_in_dim(blank, strip_cells, tile_index * strip_rows, 3)
     rim_cells = jnp.stack([first_row, placed[:, :, 0], last_row, placed[:, :, 1]], axis=2)
-    edge_set = lax.psum(rim_cells, "ty")
+    edge_set = jnp.sum(lax.all_gather(rim_cells, "ty"), axis=0)
     return edge_set
 
 

time: 606 us -> 649 us (1.071)
  other arithmetic: 126 us -> 163 us
  waiting for transfers between devices: 271 us -> 293 us
  local copies, waits for them, and re-layouts: 162 us -> 146 us
    all_gather x0 -> x3, waiting for transfers between devices: none -> 292 us  [gather_edges(): edge_set = jnp.sum(lax.all_gather(rim_cells, 'ty'), axis=0)]
    psum x3 -> x0, waiting for transfers between devices: 271 us -> none  [gather_edges(): edge_set = lax.psum(rim_cells, 'ty')]
    reduce_sum x0 -> x3, other arithmetic: none -> 29.5 us  [gather_edges(): edge_set = jnp.sum(lax.all_gather(rim_cells, 'ty'), axis=0)]
    reshape x5, local copies, waits for them, and re-layouts: 20.2 us -> 12 us  [seam_halo(): neighbor = neighbor.reshape(levels, 6, 4, row_width)]
    reshape x3 -> x0, local copies, waits for them, and re-layouts: 6.85 us -> none  [seam_halo(): flattened = edge_set.reshape(levels, 24, row_width)]
    unnamed x19 -> x21, local copies, waits for them, and re-layouts: 28.6 us -> 28.6 us
  transfers between devices with their start and end apart: 9 -> 9, of which waited for: 3 -> 3; matrix products, arithmetic and copies ran while one was open for 14% -> 17% of each run, Pallas kernels for 0% -> 0%
where the time goes in v1:
time: 649 us; the launch traced here: 639 us
  waiting for transfers between devices  293 us (45%)
  other arithmetic  163 us (25%)
  local copies, waits for them, and re-layouts  146 us (22%)
  starting transfers between devices  18.3 us (3%)
  between operations  13.8 us (2%)
    all_gather x3, waiting for transfers between devices, gather_edges(): edge_set = jnp.sum(lax.all_gather(rim_cells, 'ty'), axis=0)  292 us
    add x2, other arithmetic, laplace(): metric[0] * (padded_x[..., :-2] - source)  70.8 us
    add x1, other arithmetic, per_device(): fields - damp_four[:, None, None, None] * fourth  35.1 us
    reduce_sum x3, other arithmetic, gather_edges(): edge_set = jnp.sum(lax.all_gather(rim_cells, 'ty'), axis=0)  29.5 us
    unnamed x21, local copies, waits for them, and re-layouts  28.6 us
    slice x4, local copies, waits for them, and re-layouts, strip_edges(): east_cells = jnp.transpose(source[:, :, :, -1], (0, 2, 1))  18.6 us
    add x1, local copies, waits for them, and re-layouts, per_device(): fields - damp_four[:, None, None, None] * fourth  18.5 us
    broadcast_in_dim x6, local copies, waits for them, and re-layouts, laplace(): jnp.transpose(lax.dynamic_slice_in_dim(halo_cells[:, :, 1], row_start, st...  16 us
  transfers between devices with their start and end apart: 9, of which 3 were waited for; matrix products, arithmetic and copies ran while one was open for 17% of the time, Pallas kernels for 0%

profile of v1, /device:TPU:0, one launch (start us, length us, event | category | flops | bytes accessed | tf_op | source)
XLA Modules:
  0.0 639.4 jit_solution(6559607055131979618)
XLA Ops:
  6.5 4.6 fusion.57
  11.1 18.5 %copy.168 = f32[16,48,6,768]{3,0,2,1:T(8,128)} copy(f32[16,48,6,768]{3,1,2,0:T(8,128)} %param.5) | data formatting | bytes 28311552 | tf_op args[0]
  29.6 2.5 copy.181
  34.3 2.2 fusion.56
  36.4 2.2 pad_maximum_fusion.12
  38.7 4.7 collective-permute-start
  43.4 1.5 collective-permute-start.1
  47.1 1.5 copy.157
  48.6 96.5 %all-gather.7.cloned.1.call-done = f32[256,6,4,768]{3,0,1,2:T(8,128)} async-done(((f32[16,6,4,768]{3,0,1,2:T(8,128)}), f32[256,6,4,768]{3,0,1,2:T(8,128)}) %all-gather.7.cloned.1.call-update) | async-done | bytes 18874384 | tf_op jit(solution)/shard_map/all_gather | solution.py:41
  145.1 9.8 %reduce_sum.27 = f32[16,6,4,768]{3,0,1,2:T(8,128)} reduce(f32[16,16,6,4,768]{4,1,0,2,3:T(8,128)} %bitcast.138, f32[]{:T(128)} %constant.20.clone.1), dimensions={0}, to_apply=%region_0.1 | reduce | flops 4423680 | bytes 20054020 | tf_op jit(solution)/shard_map/reduce_sum | solution.py:41
  154.9 1.4 copy.140
  156.3 1.4 convolution_bitcast_fusion.2
  157.6 1.4 copy.180
  159.0 5.1 rev.9
  164.1 1.8 broadcast_select_fusion
  168.4 4.0 copy.146
  172.4 1.6 dynamic-slice_bitcast_fusion.4
  174.0 4.0 copy.151
  178.0 2.0 fusion.43
  180.1 35.1 %fusion.26 = f32[16,48,6,768]{3,0,2,1:T(8,128)} fusion(f32[16,48,6,768]{3,0,2,1:T(8,128)} %copy.168, f32[16,1,6,768]{3,0,2,1:T(8,128)} %get-tuple-element.38, f32[16,1,6,768]{3,0,2,1:T(8,128)} %get-tuple-element.37, f32[16,48,6,1]{3,0,2,1:T(8,128)} %copy.151, f32[16,48,6,1]{3,0,2,1:T(8,128)} %copy.146, f32[48,6,768]{2,1,0:T(8,128)} %copy.157, ...), kind=kLoop, calls=%fused_computation.35 | loop fusion | flops 53084160 | bytes 32477184 | tf_op jit(solution)/shard_map/add | solution.py:75
  215.2 5.4 fusion.55
  220.5 2.1 fusion.54
  222.6 3.4 copy.184
  226.0 3.4 copy.161
  229.5 1.5 pad_maximum_fusion.16
  231.8 1.7 dynamic_update_slice.10
  234.6 2.1 pad_maximum_fusion.13
  236.8 4.6 collective-permute-start.2
  241.4 1.3 collective-permute-start.3
  242.7 97.6 %all-gather.9.cloned.1.call-done = f32[256,6,4,768]{3,0,1,2:T(8,128)} async-done(((f32[16,6,4,768]{3,0,1,2:T(8,128)}), f32[256,6,4,768]{3,0,1,2:T(8,128)}) %all-gather.9.cloned.1.call-update) | async-done | bytes 18874384 | tf_op jit(solution)/shard_map/all_gather | solution.py:41
  340.3 9.8 %reduce_sum.28 = f32[16,6,4,768]{3,0,1,2:T(8,128)} reduce(f32[16,16,6,4,768]{4,1,0,2,3:T(8,128)} %bitcast.139, f32[]{:T(128)} %constant.20.clone.1), dimensions={0}, to_apply=%region_1.2 | reduce | flops 4423680 | bytes 20054020 | tf_op jit(solution)/shard_map/reduce_sum | solution.py:41
  350.1 1.4 copy.162
  351.5 2.3 convolution_bitcast_fusion.1
  353.8 2.7 reshape.133
  356.5 2.7 copy.164
  359.2 4.7 rev.10
  363.9 2.0 broadcast_select_fusion.1
  368.5 4.0 copy.166
  372.4 1.6 dynamic-slice_bitcast_fusion.2
  374.0 4.0 copy.167
  378.0 2.1 fusion.41
  380.1 35.7 %fusion.15 = f32[16,48,6,768]{3,0,2,1:T(8,128)} fusion(f32[16,48,6,768]{3,0,2,1:T(8,128)} %fusion.26, f32[16,1,6,768]{3,0,2,1:T(8,128)} %get-tuple-element.34, f32[16,1,6,768]{3,0,2,1:T(8,128)} %get-tuple-element.33, f32[16,48,6,1]{3,0,2,1:T(8,128)} %copy.167, f32[16,48,6,1]{3,0,2,1:T(8,128)} %copy.166, f32[48,6,768]{2,1,0:T(8,128)} %copy.157, ...), kind=kLoop, calls=%fused_computation.20 | loop fusion | flops 53084160 | bytes 32477184 | tf_op jit(solution)/shard_map/add | solution.py:75
  415.8 5.3 fusion.53
  421.1 2.1 fusion.52
  423.3 3.4 copy.169
  426.7 3.4 copy.170
  430.1 1.5 pad_maximum_fusion.17
  432.4 1.7 dynamic_update_slice.11
  435.2 2.2 pad_maximum_fusion.14
  437.4 4.6 collective-permute-start.4
  442.0 1.5 collective-permute-start.5
  443.5 98.4 %all-gather.11.cloned.1.call-done = f32[256,6,4,768]{3,0,1,2:T(8,128)} async-done(((f32[16,6,4,768]{3,0,1,2:T(8,128)}), f32[256,6,4,768]{3,0,1,2:T(8,128)}) %all-gather.11.cloned.1.call-update) | async-done | bytes 18874384 | tf_op jit(solution)/shard_map/all_gather | solution.py:41
  541.9 9.8 %reduce_sum.29 = f32[16,6,4,768]{3,0,1,2:T(8,128)} reduce(f32[16,16,6,4,768]{4,1,0,2,3:T(8,128)} %bitcast.140, f32[]{:T(128)} %constant.20.clone.1), dimensions={0}, to_apply=%region_2.3 | reduce | flops 4423680 | bytes 20054020 | tf_op jit(solution)/shard_map/reduce_sum | solution.py:41
  551.8 1.4 copy.173
  553.1 2.4 convolution_bitcast_fusion
  555.5 2.6 reshape.135
  558.1 2.7 copy.175
  560.8 4.7 rev.11
  565.5 2.0 broadcast_select_fusion.2
  569.3 3.9 copy.177
  573.2 4.0 copy.178
  577.3 1.3 fusion.39
  578.8 35.1 %fusion.4 = f32[16,48,6,768]{3,0,2,1:T(8,128)} fusion(f32[16,48,6,768]{3,0,2,1:T(8,128)} %fusion.15, f32[16,1,6,768]{3,0,2,1:T(8,128)S(1)} %get-tuple-element.30, f32[16,1,6,768]{3,0,2,1:T(8,128)S(1)} %get-tuple-element.29, f32[16,48,6,1]{3,0,2,1:T(8,128)} %copy.178, f32[16,48,6,1]{3,0,2,1:T(8,128)} %copy.177, f32[16]{0:T(128)S(1)} %copy-done.6, ...), kind=kLoop, calls=%fused_computation.5 | loop fusion | flops 67239936 | bytes 46633088 | tf_op jit(solution)/shard_map/add | solution.py:86
  613.9 18.5 %copy.179 = f32[16,48,6,768]{3,1,2,0:T(8,128)} copy(f32[16,48,6,768]{3,0,2,1:T(8,128)} %fusion.4) | data formatting | bytes 28311552 | tf_op jit(solution)/shard_map/add | solution.py:86
  (53 shorter events, 15.4 us)
Async XLA Ops:
  6.5 138.5 %all-gather.7.cloned.1.call-start = ((), (), s32[]{:S(2)}) async-start(), calls=%async_computation | async-start | bytes 20054016 | tf_op jit(solution)/shard_map/all_gather | solution.py:41
  34.3 10.6 %copy-start.5 = (s32[6,4,3]{0,1,2:T(4,128)S(1)}, s32[6,4,3]{0,1,2:T(4,128)}, u32[]{:S(2)}) copy-start(s32[6,4,3]{0,1,2:T(4,128)} %param.9) | copy-start | bytes 868
  34.3 10.9 %copy-start.4 = (f32[4,48,6,768]{3,1,2,0:T(8,128)S(1)}, f32[4,48,6,768]{3,1,2,0:T(8,128)}, u32[]{:S(2)}) copy-start(f32[4,48,6,768]{3,1,2,0:T(8,128)} %param.8) | copy-start | bytes 10616836
  38.6 301.7 %all-gather.9.cloned.1.call-start = ((), (), s32[]{:S(2)}) async-start(), calls=%async_computation.1 | async-start | bytes 20054016 | tf_op jit(solution)/shard_map/all_gather | solution.py:41
  38.7 139.4 %collective-permute-start = (f32[16,1,6,768]{3,0,2,1:T(8,128)}, f32[16,1,6,768]{3,0,2,1:T(8,128)}, u32[]{:S(2)}, u32[]{:S(2)}) collective-permute-start(f32[16,1,6,768]{3,0,2,1:T(8,128)} %get-tuple-element.17), channel_id=1, source_target_pairs={{0,1},{1,2},{2,3},{3,4},{4,5},{5,6},{6,7},{7,8},{8,9},{9,10},{10,1... | collective-permute-start | bytes 884744 | tf_op jit(solution)/shard_map/ppermute | solution.py:15
  43.4 134.7 %collective-permute-start.1 = (f32[16,1,6,768]{3,0,2,1:T(8,128)}, f32[16,1,6,768]{3,0,2,1:T(8,128)}, u32[]{:S(2)}, u32[]{:S(2)}) collective-permute-start(f32[16,1,6,768]{3,0,2,1:T(8,128)} %get-tuple-element.19), channel_id=1, source_target_pairs={{1,0},{2,1},{3,2},{4,3},{5,4},{6,5},{7,6},{8,7},{9,8},{10,9},{11,1... | collective-permute-start | bytes 884744 | tf_op jit(solution)/shard_map/ppermute | solution.py:17
  165.9 1.1 copy-start.2
  236.8 305.2 %all-gather.11.cloned.1.call-start = ((), (), s32[]{:S(2)}) async-start(), calls=%async_computation.2 | async-start | bytes 20054016 | tf_op jit(solution)/shard_map/all_gather | solution.py:41
  236.8 141.2 %collective-permute-start.2 = (f32[16,1,6,768]{3,0,2,1:T(8,128)}, f32[16,1,6,768]{3,0,2,1:T(8,128)}, u32[]{:S(2)}, u32[]{:S(2)}) collective-permute-start(f32[16,1,6,768]{3,0,2,1:T(8,128)} %get-tuple-element.11), channel_id=1, source_target_pairs={{0,1},{1,2},{2,3},{3,4},{4,5},{5,6},{6,7},{7,8},{8,9},{9,10},{10,1... | collective-permute-start | bytes 884744 | tf_op jit(solution)/shard_map/ppermute | solution.py:15
  241.4 136.6 %collective-permute-start.3 = (f32[16,1,6,768]{3,0,2,1:T(8,128)}, f32[16,1,6,768]{3,0,2,1:T(8,128)}, u32[]{:S(2)}, u32[]{:S(2)}) collective-permute-start(f32[16,1,6,768]{3,0,2,1:T(8,128)} %get-tuple-element.14), channel_id=1, source_target_pairs={{1,0},{2,1},{3,2},{4,3},{5,4},{6,5},{7,6},{8,7},{9,8},{10,9},{11,1... | collective-permute-start | bytes 884744 | tf_op jit(solution)/shard_map/ppermute | solution.py:17
  366.0 1.0 copy-start.3
  437.4 139.9 %collective-permute-start.4 = (f32[16,1,6,768]{3,0,2,1:T(8,128)}, f32[16,1,6,768]{3,0,2,1:T(8,128)}, u32[]{:S(2)}, u32[]{:S(2)}) collective-permute-start(f32[16,1,6,768]{3,0,2,1:T(8,128)} %get-tuple-element.5), channel_id=1, source_target_pairs={{0,1},{1,2},{2,3},{3,4},{4,5},{5,6},{6,7},{7,8},{8,9},{9,10},{10,1... | collective-permute-start | bytes 884744 | tf_op jit(solution)/shard_map/ppermute | solution.py:15
  442.0 135.3 %collective-permute-start.5 = (f32[16,1,6,768]{3,0,2,1:T(8,128)}, f32[16,1,6,768]{3,0,2,1:T(8,128)}, u32[]{:S(2)}, u32[]{:S(2)}) collective-permute-start(f32[16,1,6,768]{3,0,2,1:T(8,128)} %get-tuple-element.8), channel_id=1, source_target_pairs={{1,0},{2,1},{3,2},{4,3},{5,4},{6,5},{7,6},{8,7},{9,8},{10,9},{11,1... | collective-permute-start | bytes 884744 | tf_op jit(solution)/shard_map/ppermute | solution.py:17
  567.5 1.0 copy-start.1
  573.2 5.3 copy-start.6
  573.2 5.4 copy-start.7
  577.3 1.5 copy-start
Sparse Core Ops, SparseCore 0:
  38.7 106.2 all-gather.6
  236.9 103.3 all-gather.8
  437.5 104.3 all-gather.10
